TPU v7x, 128 devices: a whole 4x4x4 slice. The times are simulated.
128 devices in a mesh: dp: 16 (over y_lo, x, core), tensor: 8 (over y_hi, z).
Axes of the slice: x: 4, y: 4 (y_hi: 2, y_lo: 2; y = y_hi * 2 + y_lo), z: 4, core: 2. Of those that a mesh axis runs over, the one named last changes fastest.
Arguments:
- tokens: bfloat16 [12288, 2048], P('dp'), may hold values from -6 to 6
- cotangent: bfloat16 [12288, 2048], P('dp'), may hold values from -6 to 6
- segments: int32 [12288], replicated, may hold values from 0 to 15, never falling along the last dimension, each value on 1 to 1537 neighbouring positions
- attn_norm_gain: float32 [2048], P('dp'), may hold values from 0.5 to 1.5
- attn_norm_bias: float32 [2048], P('dp'), may hold values from -1.25 to 1.25
- query_weight: float32 [2048, 2048], P('dp', 'tensor'), may hold values from -0.125 to 0.125
- query_bias: float32 [16, 128], P('tensor', 'dp'), may hold values from -1.25 to 1.25
- kv_weight: float32 [2048, 256], P('dp'), may hold values from -0.125 to 0.125
- value_bias: float32 [128], P('dp'), may hold values from -1.25 to 1.25
- out_weight: float32 [2048, 2048], P('tensor', 'dp'), may hold values from -0.5 to 0.5
- out_bias: float32 [2048], P('dp'), may hold values from -1.25 to 1.25
- mlp_norm_gain: float32 [2048], P('dp'), may hold values from 0.5 to 1.5
- mlp_norm_bias: float32 [2048], P('dp'), may hold values from -1.25 to 1.25
- up_weight: float32 [2048, 8192], P('dp', 'tensor'), may hold values from -0.125 to 0.125
- up_bias: float32 [64, 128], P('tensor', 'dp'), may hold values from -1.25 to 1.25
- down_weight: float32 [8192, 2048], P('tensor', 'dp'), may hold values from -0.0625 to 0.0625
- down_bias: float32 [2048], P('dp'), may hold values from -1.25 to 1.25
Outputs:
- output: bfloat16 [12288, 2048], P('dp')
- input_grad: float32 [12288, 2048], P('dp')
- attn_norm_gain_grad: float32 [2048], P('dp')
- attn_norm_bias_grad: float32 [2048], P('dp')
- query_weight_grad: float32 [2048, 2048], P('dp', 'tensor')
- query_bias_grad: float32 [16, 128], P('tensor', 'dp')
- kv_weight_grad: float32 [2048, 256], P('dp')
- value_bias_grad: float32 [128], P('dp')
- out_weight_grad: float32 [2048, 2048], P('tensor', 'dp')
- out_bias_grad: float32 [2048], P('dp')
- mlp_norm_gain_grad: float32 [2048], P('dp')
- mlp_norm_bias_grad: float32 [2048], P('dp')
- up_weight_grad: float32 [2048, 8192], P('dp', 'tensor')
- up_bias_grad: float32 [64, 128], P('tensor', 'dp')
- down_weight_grad: float32 [8192, 2048], P('tensor', 'dp')
- down_bias_grad: float32 [2048], P('dp')
Inputs may be any that keep to these rules, and one draw needn't show every extreme that they name: `segments`: segment numbers never fall along the stream; every document spans 1 to 1537 consecutive tokens, and some document spans exactly 1537.
All inputs are finite; a program needn't handle non-finite values.
Results may differ from a plain program's by a relative error of at most 0.03.
Values may be sent and summed in bfloat16 or wider, within the bound.
A program may use at most 192 MiB of HBM per device.

v0:
```python
import math
import jax
import jax.numpy as jnp
from jax import lax
from jax.sharding import PartitionSpec as P

HD = 128
DOC_MOST = 2000
EPS = 1e-05
NEG = -1e30


def from_behind(value, axis, steps):
    count = lax.axis_size(axis)
    initial, last = (max(0, -steps), min(count, count - steps))
    return lax.ppermute(value, axis, [(source, source + steps) for source in range(initial, last)])


def norm_rows(values, gain, shift):
    center = values - jnp.mean(values, axis=-1, keepdims=True)
    spread = jnp.mean(center * center, axis=-1, keepdims=True)
    return center * lax.rsqrt(spread + EPS) * gain + shift


def gelu_tanh(upward):
    inner = 0.7978845608028654 * (upward + 0.044715 * upward * upward * upward)
    return 0.5 * upward * (1.0 + jnp.tanh(inner))


def matmul(left, right):
    return jnp.dot(left, right, preferred_element_type=jnp.float32)


def contract_rows(left, right):
    return lax.dot_general(
        left, right, (((0,), (0,)), ((), ())), preferred_element_type=jnp.float32
    )


def contract_cols(left, right):
    return lax.dot_general(
        left, right, (((1,), (1,)), ((), ())), preferred_element_type=jnp.float32
    )


def heads_to_rows(matrix, local_heads, tok_rows):
    return (
        matrix.reshape(tok_rows, local_heads, HD)
        .transpose(1, 0, 2)
        .reshape(local_heads * tok_rows, HD)
    )


def rows_to_heads(matrix, local_heads, tok_rows):
    return (
        matrix.reshape(local_heads, tok_rows, HD)
        .transpose(1, 0, 2)
        .reshape(tok_rows, local_heads * HD)
    )


def body(
    tokens,
    cotangent,
    segments,
    attn_norm_gain,
    attn_norm_bias,
    query_weight,
    query_bias,
    kv_weight,
    value_bias,
    out_weight,
    out_bias,
    mlp_norm_gain,
    mlp_norm_bias,
    up_weight,
    up_bias,
    down_weight,
    down_bias,
):
    dp_size = lax.axis_size("dp")
    tok_rows = tokens.shape[0]
    local_heads = query_bias.shape[0]
    reach = min((DOC_MOST - 1) // tok_rows, dp_size // 2)
    window = (reach + 1) * tok_rows
    block_index = lax.axis_index("dp")
    scale = 1.0 / math.sqrt(HD)
    bf16 = jnp.bfloat16
    f32 = jnp.float32
    gathered = (
        lax.all_gather(attn_norm_gain.astype(bf16), "dp", axis=0, tiled=True),
        lax.all_gather(attn_norm_bias.astype(bf16), "dp", axis=0, tiled=True),
        lax.all_gather(query_weight.astype(bf16), "dp", axis=0, tiled=True),
        lax.all_gather(query_bias.astype(bf16), "dp", axis=1, tiled=True),
        lax.all_gather(kv_weight.astype(bf16), "dp", axis=0, tiled=True),
        lax.all_gather(value_bias.astype(bf16), "dp", axis=0, tiled=True),
        lax.all_gather(out_weight.astype(bf16), "dp", axis=1, tiled=True),
        lax.all_gather(out_bias.astype(bf16), "dp", axis=0, tiled=True),
        lax.all_gather(mlp_norm_gain.astype(bf16), "dp", axis=0, tiled=True),
        lax.all_gather(mlp_norm_bias.astype(bf16), "dp", axis=0, tiled=True),
        lax.all_gather(up_weight.astype(bf16), "dp", axis=0, tiled=True),
        lax.all_gather(up_bias.astype(bf16), "dp", axis=1, tiled=True),
        lax.all_gather(down_weight.astype(bf16), "dp", axis=1, tiled=True),
        lax.all_gather(down_bias.astype(bf16), "dp", axis=0, tiled=True),
    )
    gain_one = gathered[0].astype(f32)
    shift_one = gathered[1].astype(f32)
    query_w = gathered[2]
    query_b = gathered[3].reshape(-1).astype(f32)
    kv_w = gathered[4]
    value_b = gathered[5].astype(f32)
    out_w = gathered[6]
    out_b = gathered[7].astype(f32)
    gain_two = gathered[8].astype(f32)
    shift_two = gathered[9].astype(f32)
    up_w = gathered[10]
    up_b = gathered[11].reshape(-1).astype(f32)
    down_w = gathered[12]
    down_b = gathered[13].astype(f32)
    inputs = tokens.astype(f32)
    normed_one, norm_one_back = jax.vjp(norm_rows, inputs, gain_one, shift_one)
    normed_one = normed_one.astype(bf16)
    query = (matmul(normed_one, query_w) + query_b).astype(bf16)
    value_shift = jnp.concatenate([jnp.zeros((HD,), f32), value_b])
    keyval = (matmul(normed_one, kv_w) + value_shift).astype(bf16)
    pieces = []
    for offset in range(reach, 0, -1):
        pieces.append(from_behind(keyval, "dp", offset))
    window_kv = jnp.concatenate(pieces + [keyval], 0)
    window_keys = window_kv[:, :HD]
    window_values = window_kv[:, HD:]
    seg_padded = jnp.concatenate([jnp.full((reach * tok_rows,), -1, jnp.int32), segments])
    key_seg = lax.dynamic_slice_in_dim(seg_padded, block_index * tok_rows, window)
    query_seg = lax.dynamic_slice_in_dim(segments, block_index * tok_rows, tok_rows)
    key_place = jnp.arange(window, dtype=jnp.int32)
    query_place = reach * tok_rows + jnp.arange(tok_rows, dtype=jnp.int32)
    allowed = (query_seg[:, None] == key_seg[None, :]) & (
        key_place[None, :] <= query_place[:, None]
    )
    allowed = jnp.tile(allowed, (local_heads, 1))
    query_rows = heads_to_rows(query, local_heads, tok_rows)
    scores = jnp.where(allowed, contract_cols(query_rows, window_keys) * scale, NEG)
    top = jnp.max(scores, axis=-1, keepdims=True)
    log_total = top + jnp.log(jnp.sum(jnp.exp(scores - top), axis=-1, keepdims=True))
    probs = jnp.exp(scores - log_total).astype(bf16)
    attended = rows_to_heads(matmul(probs, window_values), local_heads, tok_rows).astype(bf16)
    middle = inputs + lax.psum(matmul(attended, out_w), "tensor") + out_b
    normed_two, norm_two_back = jax.vjp(norm_rows, middle, gain_two, shift_two)
    normed_two = normed_two.astype(bf16)
    hidden, gelu_back = jax.vjp(gelu_tanh, matmul(normed_two, up_w) + up_b)
    hidden = hidden.astype(bf16)
    output = (
        middle
        + lax.psum(matmul(hidden, down_w).astype(jnp.bfloat16), "tensor").astype(jnp.float32)
        + down_b
    ).astype(bf16)
    down_bias_grad = jnp.sum(cotangent.astype(f32), axis=0)
    down_weight_grad = contract_rows(hidden, cotangent)
    grad_hidden = contract_cols(cotangent, down_w)
    grad_up = gelu_back(grad_hidden)[0].astype(bf16)
    up_bias_grad = jnp.sum(grad_up.astype(f32), axis=0).reshape(-1, HD)
    up_weight_grad = contract_rows(normed_two, grad_up)
    grad_norm_two = lax.psum(contract_cols(grad_up, up_w), "tensor")
    grad_middle, mlp_gain_grad, mlp_shift_grad = norm_two_back(grad_norm_two)
    grad_middle = grad_middle + cotangent.astype(f32)
    grad_attn = grad_middle.astype(bf16)
    out_bias_grad = jnp.sum(grad_attn.astype(f32), axis=0)
    out_weight_grad = contract_rows(attended, grad_attn)
    grad_attended = contract_cols(grad_attn, out_w).astype(bf16)
    grad_rows = heads_to_rows(grad_attended, local_heads, tok_rows)
    scores_again = jnp.where(allowed, contract_cols(query_rows, window_keys) * scale, NEG)
    probs_again = jnp.exp(scores_again - log_total)
    grad_probs = contract_cols(grad_rows, window_values)
    delta = jnp.sum(probs_again * grad_probs, axis=-1, keepdims=True)
    grad_scores = (probs_again * (grad_probs - delta)).astype(bf16)
    grad_query = rows_to_heads(
        matmul(grad_scores, window_keys) * scale, local_heads, tok_rows
    ).astype(bf16)
    grad_keys = contract_rows(grad_scores, query_rows) * scale
    grad_values = contract_rows(probs_again.astype(bf16), grad_rows)
    grad_window = jnp.concatenate([grad_keys, grad_values], 1)
    own_kv_grad = grad_window[reach * tok_rows :]
    for offset in range(1, reach + 1):
        piece = grad_window[(reach - offset) * tok_rows : (reach - offset + 1) * tok_rows]
        own_kv_grad = own_kv_grad + from_behind(piece.astype(jnp.bfloat16), "dp", -offset).astype(
            piece.dtype
        )
    query_part = contract_cols(grad_query, query_w)
    grad_norm_query, kv_grad_total = (
        lax.psum(query_part.astype(jnp.bfloat16), "tensor").astype(jnp.float32),
        lax.psum(own_kv_grad.astype(jnp.bfloat16), "tensor").astype(jnp.float32),
    )
    kv_grad = kv_grad_total.astype(bf16)
    value_bias_grad = jnp.sum(kv_grad[:, HD:].astype(f32), axis=0)
    kv_weight_grad = contract_rows(normed_one, kv_grad)
    query_bias_grad = jnp.sum(grad_query.astype(f32), axis=0).reshape(local_heads, HD)
    query_weight_grad = contract_rows(normed_one, grad_query)
    grad_norm_one = grad_norm_query + contract_cols(kv_grad, kv_w)
    grad_inputs, attn_gain_grad, attn_shift_grad = norm_one_back(grad_norm_one)
    input_grad = grad_middle + grad_inputs
    summed = tuple(
        (
            lax.psum_scatter(
                attn_gain_grad.astype(jnp.bfloat16), "dp", scatter_dimension=0, tiled=True
            ).astype(jnp.float32),
            lax.psum_scatter(
                attn_shift_grad.astype(jnp.bfloat16), "dp", scatter_dimension=0, tiled=True
            ).astype(jnp.float32),
            lax.psum_scatter(
                query_weight_grad.astype(jnp.bfloat16), "dp", scatter_dimension=0, tiled=True
            ).astype(jnp.float32),
            lax.psum_scatter(
                query_bias_grad.astype(jnp.bfloat16), "dp", scatter_dimension=1, tiled=True
            ).astype(jnp.float32),
            lax.psum_scatter(
                kv_weight_grad.astype(jnp.bfloat16), "dp", scatter_dimension=0, tiled=True
            ).astype(jnp.float32),
            lax.psum_scatter(
                value_bias_grad.astype(jnp.bfloat16), "dp", scatter_dimension=0, tiled=True
            ).astype(jnp.float32),
            lax.psum_scatter(
                out_weight_grad.astype(jnp.bfloat16), "dp", scatter_dimension=1, tiled=True
            ).astype(jnp.float32),
            lax.psum_scatter(
                out_bias_grad.astype(jnp.bfloat16), "dp", scatter_dimension=0, tiled=True
            ).astype(jnp.float32),
            lax.psum_scatter(
                mlp_gain_grad.astype(jnp.bfloat16), "dp", scatter_dimension=0, tiled=True
            ).astype(jnp.float32),
            lax.psum_scatter(
                mlp_shift_grad.astype(jnp.bfloat16), "dp", scatter_dimension=0, tiled=True
            ).astype(jnp.float32),
            lax.psum_scatter(
                up_weight_grad.astype(jnp.bfloat16), "dp", scatter_dimension=0, tiled=True
            ).astype(jnp.float32),
            lax.psum_scatter(
                up_bias_grad.astype(jnp.bfloat16), "dp", scatter_dimension=1, tiled=True
            ).astype(jnp.float32),
            lax.psum_scatter(
                down_weight_grad.astype(jnp.bfloat16), "dp", scatter_dimension=1, tiled=True
            ).astype(jnp.float32),
            lax.psum_scatter(
                down_bias_grad.astype(jnp.bfloat16), "dp", scatter_dimension=0, tiled=True
            ).astype(jnp.float32),
        )
    )
    return (output, input_grad) + summed


def solution(mesh):
    return jax.shard_map(
        body,
        mesh=mesh,
        in_specs=(
            P("dp", None),
            P("dp", None),
            P(),
            P("dp"),
            P("dp"),
            P("dp", "tensor"),
            P("tensor", "dp"),
            P("dp", None),
            P("dp"),
            P("tensor", "dp"),
            P("dp"),
            P("dp"),
            P("dp"),
            P("dp", "tensor"),
            P("tensor", "dp"),
            P("tensor", "dp"),
            P("dp"),
        ),
        out_specs=(
            P("dp", None),
            P("dp", None),
            P("dp"),
            P("dp"),
            P("dp", "tensor"),
            P("tensor", "dp"),
            P("dp", None),
            P("dp"),
            P("tensor", "dp"),
            P("dp"),
            P("dp"),
            P("dp"),
            P("dp", "tensor"),
            P("tensor", "dp"),
            P("tensor", "dp"),
            P("dp"),
        ),
        check_vma=False,
    )
```

profile of v0, /device:TPU:0, one launch (start us, length us, event | category | flops | bytes accessed | tf_op | source)
XLA Modules:
  0.0 1073.2 jit_solution(2823137192838508573)
XLA Ops:
  16.5 30.5 %all-reduce.2 = bf16[128]{0:T(256)(128)(2,1)S(1)} all-reduce(bf16[128]{0:T(256)(128)(2,1)S(1)} %dynamic-update-slice), channel_id=1, replica_groups=mesh['dp'=16,'tensor'=8] {'dp'}, use_global_device_ids=true, to_apply=%add.2 | all-reduce | flops 128 | bytes 512
  50.4 15.9 %all-gather.1 = bf16[16,1,128]{2,1,0:T(2,128)(2,1)S(1)} all-gather(bf16[1,1,128]{2,1,0:T(2,128)(2,1)S(1)} %convert_bitcast_fusion.5), channel_id=1, replica_groups=mesh['dp'=16,'tensor'=8] {'dp'}, dimensions={0}, use_global_device_ids=true | all-gather | bytes 4352 | tf_op jit(solution)/shard_map/all_gather | solution.py:92
  66.3 17.8 %all-gather = bf16[16,1,128]{2,1,0:T(2,128)(2,1)S(1)} all-gather(bf16[1,1,128]{2,1,0:T(2,128)(2,1)S(1)} %convert_bitcast_fusion.6), channel_id=1, replica_groups=mesh['dp'=16,'tensor'=8] {'dp'}, dimensions={0}, use_global_device_ids=true | all-gather | bytes 4352 | tf_op jit(solution)/shard_map/all_gather | solution.py:91
  84.3 3.4 fusion.8
  90.6 4.0 fusion.27
  99.5 23.1 %all-gather.2 = bf16[16,8,2]{1,2,0:T(2,128)(2,1)S(1)} all-gather(bf16[1,8,2]{1,2,0:T(2,128)(2,1)S(1)} %convert_bitcast_fusion.4), channel_id=1, replica_groups=mesh['dp'=16,'tensor'=8] {'dp'}, dimensions={0}, use_global_device_ids=true | all-gather | bytes 544 | tf_op jit(solution)/shard_map/all_gather | solution.py:94
  122.9 3.9 fusion.26
  132.4 6.7 fusion.54
  139.1 7.0 exponential_reduce_fusion
  146.1 9.8 fusion.1
  155.9 5.8 convolution_convert_fusion.7
  162.9 4.9 fusion.55
  173.6 16.2 %all-gather.5 = bf16[16,1,128]{2,1,0:T(2,128)(2,1)S(1)} all-gather(bf16[1,1,128]{2,1,0:T(2,128)(2,1)S(1)} %convert_bitcast_fusion.1), channel_id=1, replica_groups=mesh['dp'=16,'tensor'=8] {'dp'}, dimensions={0}, use_global_device_ids=true | all-gather | bytes 4352 | tf_op jit(solution)/shard_map/all_gather | solution.py:100
  191.1 17.5 %all-gather.4 = bf16[16,1,128]{2,1,0:T(2,128)(2,1)S(1)} all-gather(bf16[1,1,128]{2,1,0:T(2,128)(2,1)S(1)} %convert_bitcast_fusion.2), channel_id=1, replica_groups=mesh['dp'=16,'tensor'=8] {'dp'}, dimensions={0}, use_global_device_ids=true | all-gather | bytes 4352 | tf_op jit(solution)/shard_map/all_gather | solution.py:99
  209.8 16.2 %all-gather.3 = bf16[16,1,128]{2,1,0:T(2,128)(2,1)S(1)} all-gather(bf16[1,1,128]{2,1,0:T(2,128)(2,1)S(1)} %convert_bitcast_fusion.3), channel_id=1, replica_groups=mesh['dp'=16,'tensor'=8] {'dp'}, dimensions={0}, use_global_device_ids=true | all-gather | bytes 4352 | tf_op jit(solution)/shard_map/all_gather | solution.py:98
  226.6 19.9 %all_gather.53 = bf16[8,128]{0,1:T(8,128)(2,1)} all-gather(bf16[8,8]{0,1:T(8,128)(2,1)} %copy.55), channel_id=1, replica_groups=mesh['dp'=16,'tensor'=8] {'dp'}, dimensions={1}, use_global_device_ids=true | all-gather | bytes 2176 | tf_op jit(solution)/shard_map/all_gather | solution.py:102
  249.1 65.9 %all-reduce.18.cloned.1.call-done = f32[768,2048]{1,0:T(8,128)} async-done(((f32[768,2048]{1,0:T(8,128)}), f32[768,2048]{1,0:T(8,128)}) %all-reduce.18.cloned.1.call-update) | async-done | bytes 6291472 | tf_op jit(solution)/shard_map/psum | solution.py:147
  315.0 3.7 fusion.50
  323.4 28.4 %all-gather.19.cloned.1.call-done = bf16[2048,1024]{1,0:T(8,128)(2,1)} async-done(((bf16[128,1024]{1,0:T(8,128)(2,1)}), bf16[2048,1024]{1,0:T(8,128)(2,1)}) %all-gather.19.cloned.1.call-update) | async-done | bytes 4194320 | tf_op jit(solution)/shard_map/all_gather | solution.py:101
  351.7 9.2 fusion.43
  360.9 37.9 %all-gather.21.cloned.1.call-done = bf16[1024,2048]{1,0:T(8,128)(2,1)} async-done(((bf16[1024,128]{1,0:T(8,128)(2,1)}), bf16[1024,2048]{1,0:T(8,128)(2,1)}) %all-gather.21.cloned.1.call-update) | async-done | bytes 4194320 | tf_op jit(solution)/shard_map/all_gather | solution.py:103
  398.8 10.6 fusion.45
  410.5 5.4 fusion.56
  416.2 8.7 convolution_convert_fusion
  424.9 6.5 copy.65
  431.5 131.4 %all-reduce.20.cloned.1.call-done = f32[768,2048]{1,0:T(8,128)} async-done(((f32[768,2048]{1,0:T(8,128)}), f32[768,2048]{1,0:T(8,128)}) %all-reduce.20.cloned.1.call-update) | async-done | bytes 6291472 | tf_op jit(solution)/shard_map/psum | solution.py:163
  562.9 6.5 multiply_reduce_fusion.1
  569.5 4.4 fusion.49
  582.5 9.2 convolution_convert_fusion.1
  592.0 4.0 convolution_convert_fusion.8
  597.3 13.0 %multiply_reduce_fusion = (f32[1536]{0:T(1024)S(1)}, f32[1536,2304]{1,0:T(8,128)}) fusion(f32[1536,2304]{1,0:T(8,128)} %get-tuple-element.49, f32[1536]{0:T(1024)S(1)} %log_add_fusion, bf16[1536,128]{1,0:T(8,128)(2,1)S(1)} %bitcast.99, bf16[2304,256]{1,0:T(8,128)(2,1)} %copy-done.10), kind=kOutput, calls=%fused_computation.3 | convolution fusion | flops 916584960 | bytes 29306880 | tf_op jit(solution)/shard_map/dot_general | solution.py:41
  611.6 7.3 multiply_convert_fusion
  619.0 3.1 fusion.24
  624.0 3.9 convolution_convert_fusion.6
  627.9 5.3 fusion.57
  633.2 5.2 convolution_multiply_fusion.1
  643.5 7.5 convolution_convert_fusion.3
  653.8 6.0 collective-permute-done.3
  662.1 17.5 %all-gather.6 = bf16[16,1,128]{2,1,0:T(2,128)(2,1)S(1)} all-gather(bf16[1,1,128]{2,1,0:T(2,128)(2,1)S(1)} %convert_bitcast_fusion), channel_id=1, replica_groups=mesh['dp'=16,'tensor'=8] {'dp'}, dimensions={0}, use_global_device_ids=true | all-gather | bytes 4352 | tf_op jit(solution)/shard_map/all_gather | solution.py:104
  682.2 9.6 reduce-scatter.18.cloned.1.call-done
  693.4 66.8 %reduce-scatter.16.cloned.1.call-done = bf16[128,1024]{1,0:T(8,128)(2,1)} async-done(((bf16[2048,1024]{1,0:T(8,128)(2,1)}), bf16[128,1024]{1,0:T(8,128)(2,1)}) %reduce-scatter.16.cloned.1.call-update) | async-done | bytes 262160 | tf_op jit(solution)/shard_map/reduce_scatter | solution.py:233
  762.0 60.6 %reduce-scatter.12.cloned.1.call-done = bf16[128,256]{1,0:T(8,128)(2,1)} async-done(((bf16[2048,256]{1,0:T(8,128)(2,1)}), bf16[128,256]{1,0:T(8,128)(2,1)}) %reduce-scatter.12.cloned.1.call-update) | async-done | bytes 65552 | tf_op jit(solution)/shard_map/reduce_scatter | solution.py:209
  824.1 154.3 %all-reduce.22.cloned.1.call-done = (bf16[768,2048]{1,0:T(8,128)(2,1)}, bf16[768,2048]{1,0:T(8,128)(2,1)}, bf16[768,256]{0,1:T(8,128)(2,1)}) async-done(((bf16[768,2048]{1,0:T(8,128)(2,1)}, bf16[768,2048]{1,0:T(8,128)(2,1)}, bf16[768,256]{0,1:T(8,128)(2,1)}), (bf16[768,2048]{1,0:T(8,128)(2,1)}, bf16[768,2048]{1,0:T(8,128)(2,1)}, bf16[768,256]{0,1:T(8,128)(2,1)})) %all-reduce.22.cloned.1.call-update) | async-done | bytes 6684688 | tf_op jit(solution)/shard_map/psum | solution.py:154
  978.3 3.9 convolution_convert_fusion.5
  983.4 4.7 fusion.44
  991.1 55.5 %all-reduce.12 = (bf16[2048]{0:T(1024)(128)(2,1)S(1)}, bf16[2048]{0:T(1024)(128)(2,1)S(1)}, bf16[2,128]{1,0:T(2,128)(2,1)S(1)}, bf16[128]{0:T(256)(128)(2,1)S(1)...) all-reduce(bf16[2048]{0:T(1024)(128)(2,1)S(1)} %get-tuple-element.1, ...), channel_id=2, replica_groups=mesh['dp'=16,'tensor'=8] {'dp'}, use_global_device_ids=true, to_apply=%region_17.18.clone | all-reduce | flops 13696 | bytes 54784
  1050.3 6.8 add_convert_fusion
  1058.8 5.8 add_add_fusion.2
  (216 shorter events, 84.9 us)
Async XLA Ops:
  7.2 42.2 %copy-start.1 = (bf16[768,2048]{1,0:T(8,128)(2,1)S(1)}, bf16[768,2048]{1,0:T(8,128)(2,1)}, u32[]{:S(2)}) copy-start(bf16[768,2048]{1,0:T(8,128)(2,1)} %param.17) | copy-start | bytes 9437188
  7.2 76.9 %copy-start.25 = (s32[12288]{0:T(1024)S(1)}, s32[12288]{0:T(1024)}, u32[]{:S(2)}) copy-start(s32[12288]{0:T(1024)} %param.19) | copy-start | bytes 147460
  7.2 83.4 %all-gather.15.cloned.1.call-start = ((), (), s32[]{:S(2)}) async-start(), calls=%async_computation.6 | async-start | bytes 1114112 | tf_op jit(solution)/shard_map/all_gather | solution.py:95
  9.0 114.0 %all-gather.13.cloned.1.call-start = ((), (), s32[]{:S(2)}) async-start(), calls=%async_computation.5 | async-start | bytes 1114112 | tf_op jit(solution)/shard_map/all_gather | solution.py:93
  10.6 152.3 %all-gather.17.cloned.1.call-start = ((), (), s32[]{:S(2)}) async-start(), calls=%async_computation.7 | async-start | bytes 1114112 | tf_op jit(solution)/shard_map/all_gather | solution.py:97
  12.2 302.8 %all-reduce.18.cloned.1.call-start = ((), (), s32[]{:S(2)}) async-start(), calls=%async_computation.8 | async-start | bytes 12582912 | tf_op jit(solution)/shard_map/psum | solution.py:147
  49.4 38.3 %copy-start.18 = (f32[768]{0:T(1024)}, f32[768]{0:T(1024)S(1)}, u32[]{:S(2)}) copy-start(f32[768]{0:T(1024)S(1)} %broadcast_multiply_fusion.1) | copy-start | bytes 9220
  50.4 37.3 %copy-start.27 = (f32[768]{0:T(1024)}, f32[768]{0:T(1024)S(1)}, u32[]{:S(2)}) copy-start(f32[768]{0:T(1024)S(1)} %fusion.12) | copy-start | bytes 9220
  50.4 37.3 %copy-start.23 = (f32[768]{0:T(1024)}, f32[768]{0:T(1024)S(1)}, u32[]{:S(2)}) copy-start(f32[768]{0:T(1024)S(1)} %fusion.37) | copy-start | bytes 9220
  90.6 8.9 copy-start.42
  94.5 33.6 %collective-permute-start.1 = (bf16[768,256]{1,0:T(8,128)(2,1)}, bf16[768,256]{1,0:T(8,128)(2,1)}, u32[]{:S(2)}, u32[]{:S(2)}) collective-permute-start(bf16[768,256]{1,0:T(8,128)(2,1)} %fusion.27), channel_id=1, source_target_pairs={{0,8},{8,16},{16,24},{24,32},{32,40},{40,48},{48,56},{56,64},{64,7... | collective-permute-start | bytes 1179656 | tf_op jit(solution)/shard_map/ppermute | solution.py:16
  97.5 30.6 %collective-permute-start = (bf16[768,256]{1,0:T(8,128)(2,1)}, bf16[768,256]{1,0:T(8,128)(2,1)}, u32[]{:S(2)}, u32[]{:S(2)}) collective-permute-start(bf16[768,256]{1,0:T(8,128)(2,1)} %fusion.27), channel_id=1, source_target_pairs={{0,16},{8,24},{16,32},{24,40},{32,48},{40,56},{48,64},{56,72},{64,... | collective-permute-start | bytes 1179656 | tf_op jit(solution)/shard_map/ppermute | solution.py:16
  128.1 11.0 %copy-start.13 = (bf16[768,2,128]{2,0,1:T(8,128)(2,1)}, bf16[768,2,128]{2,0,1:T(8,128)(2,1)S(1)}, u32[]{:S(2)}) copy-start(bf16[768,2,128]{2,0,1:T(8,128)(2,1)S(1)} %copy.53) | copy-start | bytes 1179652
  129.6 9.5 copy-start.10
  167.9 183.9 %all-gather.19.cloned.1.call-start = ((), (), s32[]{:S(2)}) async-start(), calls=%async_computation.9 | async-start | bytes 4456448 | tf_op jit(solution)/shard_map/all_gather | solution.py:101
  169.7 229.1 %all-gather.21.cloned.1.call-start = ((), (), s32[]{:S(2)}) async-start(), calls=%async_computation.10 | async-start | bytes 4456448 | tf_op jit(solution)/shard_map/all_gather | solution.py:103
  171.6 391.3 %all-reduce.20.cloned.1.call-start = ((), (), s32[]{:S(2)}) async-start(), calls=%async_computation.11 | async-start | bytes 12582912 | tf_op jit(solution)/shard_map/psum | solution.py:163
  398.8 11.7 %copy-start.41 = (bf16[2048,1024]{1,0:T(8,128)(2,1)S(1)}, bf16[2048,1024]{1,0:T(8,128)(2,1)}, u32[]{:S(2)}) copy-start(bf16[2048,1024]{1,0:T(8,128)(2,1)} %all-gather.19.cloned.1.call-done) | copy-start | bytes 12582916
  415.9 264.3 %reduce-scatter.20.cloned.1.call-start = ((), (), s32[]{:S(2)}) async-start(), calls=%async_computation.16 | async-start | bytes 4456448
  431.4 260.3 %reduce-scatter.18.cloned.1.call-start = ((), (), s32[]{:S(2)}) async-start(), calls=%async_computation.15 | async-start | bytes 1114112
  562.9 6.5 copy-start.30
  562.9 6.5 copy-start.3
  562.9 6.6 copy-start.20
  562.9 6.6 copy-start.22
  562.9 6.6 copy-start.26
  582.5 177.7 %reduce-scatter.16.cloned.1.call-start = ((), (), s32[]{:S(2)}) async-start(), calls=%async_computation.14 | async-start | bytes 4456448 | tf_op jit(solution)/shard_map/reduce_scatter | solution.py:233
  591.7 230.8 %reduce-scatter.12.cloned.1.call-start = ((), (), s32[]{:S(2)}) async-start(), calls=%async_computation.12 | async-start | bytes 1114112 | tf_op jit(solution)/shard_map/reduce_scatter | solution.py:209
  597.2 13.1 %slice-start = ((s8[14155776]{0:T(1024)(128)(4,1)}), s8[4194304]{0:T(1024)(128)(4,1)S(1)}, s32[]{:S(2)}) async-start(s8[14155776]{0:T(1024)(128)(4,1)} %bitcast.92), calls=%async_computation.18 | async-start | bytes 8388608
  597.2 13.1 %slice-start.1 = ((s8[14155776]{0:T(1024)(128)(4,1)}), s8[4194304]{0:T(1024)(128)(4,1)S(1)}, s32[]{:S(2)}) async-start(s8[14155776]{0:T(1024)(128)(4,1)} %bitcast.92), calls=%async_computation.19 | async-start | bytes 8388608
  597.2 13.8 %slice-start.2 = ((s8[14155776]{0:T(1024)(128)(4,1)}), s8[4194304]{0:T(1024)(128)(4,1)S(1)}, s32[]{:S(2)}) async-start(s8[14155776]{0:T(1024)(128)(4,1)} %bitcast.92), calls=%async_computation.20 | async-start | bytes 8388608
  597.3 14.4 %slice-start.3 = ((s8[14155776]{0:T(1024)(128)(4,1)}), s8[1572864]{0:T(1024)(128)(4,1)S(1)}, s32[]{:S(2)}) async-start(s8[14155776]{0:T(1024)(128)(4,1)} %bitcast.92), calls=%async_computation.21 | async-start | bytes 3145728
  611.6 7.3 copy-start.11
  627.9 5.3 copy-start.14
  638.4 5.1 copy-start.37
  638.5 339.9 %all-reduce.22.cloned.1.call-start = ((), (), s32[]{:S(2)}) async-start(), calls=%async_computation.17 | async-start | bytes 13369344 | tf_op jit(solution)/shard_map/psum | solution.py:154
  640.5 13.3 %collective-permute-start.2 = (bf16[768,256]{0,1:T(8,128)(2,1)S(1)}, bf16[768,256]{0,1:T(8,128)(2,1)S(1)}, u32[]{:S(2)}, u32[]{:S(2)}) collective-permute-start(bf16[768,256]{0,1:T(8,128)(2,1)S(1)} %get-tuple-element.44), channel_id=1, source_target_pairs={{8,0},{16,8},{24,16},{32,24},{40,32},{48,40},{56,48},{64,56},{72,6... | collective-permute-start | bytes 1179656 | tf_op jit(solution)/shard_map/ppermute | solution.py:16
  641.8 9.2 copy-start.16
  641.8 9.2 copy-start.17
  641.8 17.9 %collective-permute-start.3 = (bf16[768,256]{0,1:T(8,128)(2,1)S(1)}, bf16[768,256]{0,1:T(8,128)(2,1)S(1)}, u32[]{:S(2)}, u32[]{:S(2)}) collective-permute-start(bf16[768,256]{0,1:T(8,128)(2,1)S(1)} %get-tuple-element.45), channel_id=1, source_target_pairs={{16,0},{24,8},{32,16},{40,24},{48,32},{56,40},{64,48},{72,56},{80,... | collective-permute-start | bytes 1179656 | tf_op jit(solution)/shard_map/ppermute | solution.py:16
  651.0 8.7 copy-start.6
  651.0 8.7 copy-start.9
  660.6 18.9 %copy-start.15 = (bf16[1536,128]{1,0:T(8,128)(2,1)S(1)}, bf16[1536,128]{1,0:T(8,128)(2,1)}, u32[]{:S(2)}) copy-start(bf16[1536,128]{1,0:T(8,128)(2,1)} %fusion.24) | copy-start | bytes 1179652
  660.7 404.0 %reduce-scatter.14.cloned.1.call-start = ((), (), s32[]{:S(2)}) async-start(), calls=%async_computation.13 | async-start | bytes 1114112 | tf_op jit(solution)/shard_map/reduce_scatter | solution.py:215
  762.0 221.4 %copy-start.19 = (f32[768]{0:T(1024)S(1)}, f32[768]{0:T(1024)}, u32[]{:S(2)}) copy-start(f32[768]{0:T(1024)} %copy-done.18) | copy-start | bytes 9220
  1050.3 6.8 slice-start.4
  1050.3 6.8 slice-start.5
  1050.3 8.5 copy-start.5
  1050.3 8.5 copy-start.32
  (20 other events, 59.0 us)
Sparse Core Ops, SparseCore 0:
  10.3 34.8 all-gather.14
  47.5 32.4 all-gather.12
  82.2 38.0 all-gather.16
  168.0 146.9 all-reduce.17
  317.2 34.5 all-gather.18
  353.8 44.9 all-gather.20
  416.1 146.8 all-reduce.19
  565.3 64.0 reduce-scatter.19
  631.8 59.9 reduce-scatter.17
  694.1 66.0 reduce-scatter.15
  762.7 59.8 reduce-scatter.11
  825.2 153.0 all-reduce.21
  983.5 58.6 reduce-scatter.13
where the time goes:
time: 1080 us; the launch traced here: 1070 us
  waiting for transfers between devices  561 us (52%)
  blocking collectives  230 us (21%)
  matrix products  124 us (11%)
  other arithmetic  99.1 us (9%)
  local copies, waits for them, and re-layouts  33.2 us (3%)
  between operations  17.2 us (2%)
    psum x1, waiting for transfers between devices, body(): lax.psum(matmul(hidden, down_w).astype(jnp.bfloat16), 'tensor')  154 us
    psum x1, waiting for transfers between devices, body(): grad_norm_two = lax.psum(contract_cols(grad_up, up_w), 'tensor')  131 us
    unnamed x2, blocking collectives  86 us
    reduce_scatter x1, waiting for transfers between devices, body(): lax.psum_scatter(up_weight_grad.astype(jnp.bfloat16), 'dp', scatter_dimen...  66.8 us
    psum x1, waiting for transfers between devices, body(): middle = inputs + lax.psum(matmul(attended, out_w), 'tensor') + out_b  65.9 us
    reduce_scatter x1, waiting for transfers between devices, body(): lax.psum_scatter(query_weight_grad.astype(jnp.bfloat16), 'dp', scatter_di...  60.6 us
    dot_general x7, matrix products, contract_cols(): lax.dot_general(left, right, (((1,), (1,)), ((), ())), preferred_element_...  47.1 us
    dot_general x7, matrix products, matmul(): return jnp.dot(left, right, preferred_element_type=jnp.float32)  38.4 us
  transfers between devices with their start and end apart: 17, of which 9 were waited for; matrix products, arithmetic and copies ran while one was open for 20% of the time, Pallas kernels for 0%

commit v1 on v0

--- a/solution.py
+++ b/solution.py
@@ -144,7 +144,7 @@
     log_total = top + jnp.log(jnp.sum(jnp.exp(scores - top), axis=-1, keepdims=True))
     probs = jnp.exp(scores - log_total).astype(bf16)
     attended = rows_to_heads(matmul(probs, window_values), local_heads, tok_rows).astype(bf16)
-    middle = inputs + lax.psum(matmul(attended, out_w), "tensor") + out_b
+    middle = inputs + jnp.sum(lax.all_gather(matmul(attended, out_w), "tensor"), axis=0) + out_b
     normed_two, norm_two_back = jax.vjp(norm_rows, middle, gain_two, shift_two)
     normed_two = normed_two.astype(bf16)
     hidden, gelu_back = jax.vjp(gelu_tanh, matmul(normed_two, up_w) + up_b)

time: 1080 us -> 1460 us (1.35)
  waiting for transfers between devices: 561 us -> 933 us
  other arithmetic: 99.1 us -> 116 us
    all_gather x0 -> x1, waiting for transfers between devices: none -> 413 us  [body(): lax.all_gather(matmul(attended, out_w), 'tensor')]
    psum x1 -> x0, waiting for transfers between devices: 65.9 us -> none  [body(): middle = inputs + lax.psum(matmul(attended, out_w), 'tensor') + out_b]
    unnamed x15, waiting for transfers between devices: 9.8 us -> 63 us
    reduce_scatter x1, waiting for transfers between devices: 66.8 us -> 23.7 us  [body(): lax.psum_scatter(up_weight_grad.astype(jnp.bfloat16), 'dp', scatter_dimen...]
    reduce_scatter x1, waiting for transfers between devices: 0.01 us -> 40.6 us  [body(): lax.psum_scatter(kv_weight_grad.astype(jnp.bfloat16), 'dp', scatter_dimen...]
    reduce_sum x0 -> x1, other arithmetic: none -> 20.7 us  [body(): jnp.sum(lax.all_gather(matmul(attended, out_w), 'tensor'), axis=0)]
    all_gather x1, waiting for transfers between devices: 28.4 us -> 8.63 us  [body(): lax.all_gather(up_weight.astype(bf16), 'dp', axis=0, tiled=True)]
  transfers between devices with their start and end apart: 17 -> 17, of which waited for: 9 -> 10; matrix products, arithmetic and copies ran while one was open for 20% -> 15% of each run, Pallas kernels for 0% -> 0%
where the time goes in v1:
time: 1460 us; the launch traced here: 1450 us
  waiting for transfers between devices  933 us (64%)
  blocking collectives  229 us (16%)
  matrix products  121 us (8%)
  other arithmetic  116 us (8%)
  local copies, waits for them, and re-layouts  26.9 us (2%)
  between operations  17.2 us (1%)
    all_gather x1, waiting for transfers between devices, body(): lax.all_gather(matmul(attended, out_w), 'tensor')  413 us
    psum x1, waiting for transfers between devices, body(): lax.psum(matmul(hidden, down_w).astype(jnp.bfloat16), 'tensor')  154 us
    psum x1, waiting for transfers between devices, body(): grad_norm_two = lax.psum(contract_cols(grad_up, up_w), 'tensor')  122 us
    unnamed x2, blocking collectives  83.7 us
    unnamed x15, waiting for transfers between devices  63 us
    reduce_scatter x1, waiting for transfers between devices, body(): lax.psum_scatter(query_weight_grad.astype(jnp.bfloat16), 'dp', scatter_di...  60.8 us
    dot_general x7, matrix products, contract_cols(): lax.dot_general(left, right, (((1,), (1,)), ((), ())), preferred_element_...  42.4 us
    reduce_scatter x1, waiting for transfers between devices, body(): lax.psum_scatter(kv_weight_grad.astype(jnp.bfloat16), 'dp', scatter_dimen...  40.6 us
  transfers between devices with their start and end apart: 17, of which 10 were waited for; matrix products, arithmetic and copies ran while one was open for 15% of the time, Pallas kernels for 0%

profile of v1, /device:TPU:0, one launch (start us, length us, event | category | flops | bytes accessed | tf_op | source)
XLA Modules:
  0.0 1450.6 jit_solution(161562398838563906)
XLA Ops:
  16.3 19.6 %all-gather.1 = bf16[16,1,128]{2,1,0:T(2,128)(2,1)S(1)} all-gather(bf16[1,1,128]{2,1,0:T(2,128)(2,1)S(1)} %convert_bitcast_fusion.6), channel_id=1, replica_groups=mesh['dp'=16,'tensor'=8] {'dp'}, dimensions={0}, use_global_device_ids=true | all-gather | bytes 4352 | tf_op jit(solution)/shard_map/all_gather | solution.py:91
  36.0 16.1 %all-gather.2 = bf16[16,1,128]{2,1,0:T(2,128)(2,1)S(1)} all-gather(bf16[1,1,128]{2,1,0:T(2,128)(2,1)S(1)} %convert_bitcast_fusion.5), channel_id=1, replica_groups=mesh['dp'=16,'tensor'=8] {'dp'}, dimensions={0}, use_global_device_ids=true | all-gather | bytes 4352 | tf_op jit(solution)/shard_map/all_gather | solution.py:92
  53.6 28.8 %all-reduce.2 = bf16[128]{0:T(256)(128)(2,1)S(1)} all-reduce(bf16[128]{0:T(256)(128)(2,1)S(1)} %dynamic-update-slice), channel_id=1, replica_groups=mesh['dp'=16,'tensor'=8] {'dp'}, use_global_device_ids=true, to_apply=%add.2 | all-reduce | flops 128 | bytes 512
  88.9 3.9 fusion.27
  96.9 22.3 %all-gather.3 = bf16[16,8,2]{1,2,0:T(2,128)(2,1)S(1)} all-gather(bf16[1,8,2]{1,2,0:T(2,128)(2,1)S(1)} %convert_bitcast_fusion.4), channel_id=1, replica_groups=mesh['dp'=16,'tensor'=8] {'dp'}, dimensions={0}, use_global_device_ids=true | all-gather | bytes 544 | tf_op jit(solution)/shard_map/all_gather | solution.py:94
  119.5 3.9 fusion.26
  128.9 6.8 fusion.54
  135.8 7.0 exponential_reduce_fusion
  142.8 9.8 fusion.1
  152.6 5.8 convolution_convert_fusion.7
  159.6 5.1 fusion.55
  168.5 16.0 %all-gather.4 = bf16[16,1,128]{2,1,0:T(2,128)(2,1)S(1)} all-gather(bf16[1,1,128]{2,1,0:T(2,128)(2,1)S(1)} %convert_bitcast_fusion.3), channel_id=1, replica_groups=mesh['dp'=16,'tensor'=8] {'dp'}, dimensions={0}, use_global_device_ids=true | all-gather | bytes 4352 | tf_op jit(solution)/shard_map/all_gather | solution.py:98
  184.6 17.6 %all-gather.5 = bf16[16,1,128]{2,1,0:T(2,128)(2,1)S(1)} all-gather(bf16[1,1,128]{2,1,0:T(2,128)(2,1)S(1)} %convert_bitcast_fusion.2), channel_id=1, replica_groups=mesh['dp'=16,'tensor'=8] {'dp'}, dimensions={0}, use_global_device_ids=true | all-gather | bytes 4352 | tf_op jit(solution)/shard_map/all_gather | solution.py:99
  202.2 16.1 %all-gather.6 = bf16[16,1,128]{2,1,0:T(2,128)(2,1)S(1)} all-gather(bf16[1,1,128]{2,1,0:T(2,128)(2,1)S(1)} %convert_bitcast_fusion.1), channel_id=1, replica_groups=mesh['dp'=16,'tensor'=8] {'dp'}, dimensions={0}, use_global_device_ids=true | all-gather | bytes 4352 | tf_op jit(solution)/shard_map/all_gather | solution.py:100
  218.5 18.6 %all_gather.61 = bf16[8,128]{0,1:T(8,128)(2,1)S(1)} all-gather(bf16[8,8]{0,1:T(8,128)(2,1)S(1)} %copy.55), channel_id=1, replica_groups=mesh['dp'=16,'tensor'=8] {'dp'}, dimensions={1}, use_global_device_ids=true | all-gather | bytes 2176 | tf_op jit(solution)/shard_map/all_gather | solution.py:102
  237.1 413.5 %all-gather.25.cloned.1.call-done = f32[6144,2048]{1,0:T(8,128)} async-done(((f32[768,2048]{1,0:T(8,128)}), f32[6144,2048]{1,0:T(8,128)}) %all-gather.25.cloned.1.call-update) | async-done | bytes 50331664 | tf_op jit(solution)/shard_map/all_gather | solution.py:147
  650.6 20.7 %reduce_sum.230 = f32[768,2048]{1,0:T(8,128)} reduce(f32[8,768,2048]{2,1,0:T(8,128)} %bitcast.95, f32[]{:T(128)} %constant.46.clone.1), dimensions={0}, to_apply=%region_4.5 | reduce | flops 11010048 | bytes 56623108 | tf_op jit(solution)/shard_map/reduce_sum | solution.py:147
  671.3 3.8 fusion.50
  678.5 8.6 all-gather.21.cloned.1.call-done
  687.2 9.1 fusion.43
  696.3 37.9 %all-gather.23.cloned.1.call-done = bf16[1024,2048]{1,0:T(8,128)(2,1)} async-done(((bf16[1024,128]{1,0:T(8,128)(2,1)}), bf16[1024,2048]{1,0:T(8,128)(2,1)}) %all-gather.23.cloned.1.call-update) | async-done | bytes 4194320 | tf_op jit(solution)/shard_map/all_gather | solution.py:103
  734.3 10.5 fusion.45
  746.0 5.4 fusion.56
  751.6 8.7 convolution_convert_fusion
  760.4 6.5 copy.65
  767.0 9.0 convolution_convert_fusion.1
  776.1 122.3 %all-reduce.17.cloned.1.call-done = f32[768,2048]{1,0:T(8,128)} async-done(((f32[768,2048]{1,0:T(8,128)}), f32[768,2048]{1,0:T(8,128)}) %all-reduce.17.cloned.1.call-update) | async-done | bytes 6291472 | tf_op jit(solution)/shard_map/psum | solution.py:163
  898.4 6.5 multiply_reduce_fusion.1
  904.9 4.4 fusion.49
  914.9 4.0 convolution_convert_fusion.4
  921.2 10.5 multiply_reduce_fusion
  932.0 10.6 multiply_convert_fusion
  947.6 4.0 convolution_convert_fusion.6
  951.6 5.3 fusion.57
  956.9 5.4 convolution_multiply_fusion.1
  967.3 7.4 convolution_convert_fusion.3
  977.4 8.0 collective-permute-done.3
  987.7 18.7 %all-gather.7 = bf16[16,1,128]{2,1,0:T(2,128)(2,1)S(1)} all-gather(bf16[1,1,128]{2,1,0:T(2,128)(2,1)S(1)} %convert_bitcast_fusion), channel_id=1, replica_groups=mesh['dp'=16,'tensor'=8] {'dp'}, dimensions={0}, use_global_device_ids=true | all-gather | bytes 4352 | tf_op jit(solution)/shard_map/all_gather | solution.py:104
  1009.1 23.7 %reduce-scatter.16.cloned.1.call-done = bf16[128,1024]{1,0:T(8,128)(2,1)} async-done(((bf16[2048,1024]{1,0:T(8,128)(2,1)}), bf16[128,1024]{1,0:T(8,128)(2,1)}) %reduce-scatter.16.cloned.1.call-update) | async-done | bytes 262160 | tf_op jit(solution)/shard_map/reduce_scatter | solution.py:233
  1034.5 62.7 %reduce-scatter.18.cloned.1.call-done = bf16[128,256]{1,0:T(8,128)(2,1)} async-done(((bf16[2048,256]{1,0:T(8,128)(2,1)}), bf16[128,256]{1,0:T(8,128)(2,1)}) %reduce-scatter.18.cloned.1.call-update) | async-done | bytes 65552
  1098.9 60.8 %reduce-scatter.12.cloned.1.call-done = bf16[128,256]{1,0:T(8,128)(2,1)} async-done(((bf16[2048,256]{1,0:T(8,128)(2,1)}), bf16[128,256]{1,0:T(8,128)(2,1)}) %reduce-scatter.12.cloned.1.call-update) | async-done | bytes 65552 | tf_op jit(solution)/shard_map/reduce_scatter | solution.py:209
  1161.2 154.4 %all-reduce.19.cloned.1.call-done = (bf16[768,2048]{1,0:T(8,128)(2,1)}, bf16[768,2048]{1,0:T(8,128)(2,1)}, bf16[768,256]{0,1:T(8,128)(2,1)}) async-done(((bf16[768,2048]{1,0:T(8,128)(2,1)}, bf16[768,2048]{1,0:T(8,128)(2,1)}, bf16[768,256]{0,1:T(8,128)(2,1)}), (bf16[768,2048]{1,0:T(8,128)(2,1)}, bf16[768,2048]{1,0:T(8,128)(2,1)}, bf16[768,256]{0,1:T(8,128)(2,1)})) %all-reduce.19.cloned.1.call-update) | async-done | bytes 6684688 | tf_op jit(solution)/shard_map/psum | solution.py:154
  1316.6 4.0 convolution_convert_fusion.5
  1320.7 4.7 fusion.44
  1328.4 54.9 %all-reduce.12 = (bf16[2048]{0:T(1024)(128)(2,1)S(1)}, bf16[2048]{0:T(1024)(128)(2,1)S(1)}, bf16[2,128]{1,0:T(2,128)(2,1)S(1)}, bf16[128]{0:T(256)(128)(2,1)S(1)...) all-reduce(bf16[2048]{0:T(1024)(128)(2,1)S(1)} %get-tuple-element.1, ...), channel_id=3, replica_groups=mesh['dp'=16,'tensor'=8] {'dp'}, use_global_device_ids=true, to_apply=%region_17.18.clone | all-reduce | flops 13696 | bytes 54784
  1387.1 6.9 add_convert_fusion
  1395.6 5.8 add_add_fusion.2
  1401.5 40.6 %reduce-scatter.14.cloned.1.call-done = bf16[128,256]{1,0:T(8,128)(2,1)} async-done(((bf16[2048,256]{1,0:T(8,128)(2,1)}), bf16[128,256]{1,0:T(8,128)(2,1)}) %reduce-scatter.14.cloned.1.call-update) | async-done | bytes 65552 | tf_op jit(solution)/shard_map/reduce_scatter | solution.py:215
  (216 shorter events, 76.4 us)
Async XLA Ops:
  7.2 44.9 %copy-start.37 = (u32[128]{0:T(128)S(1)}, u32[128]{0:T(128)}, u32[]{:S(2)}) copy-start(u32[128]{0:T(128)} %constant.67) | copy-start | bytes 1540
  7.2 7.5 copy-start.1
  7.2 8.5 copy-start.41
  7.2 28.7 %copy-start.42 = (f32[128]{0:T(128)S(1)}, f32[128]{0:T(128)}, u32[]{:S(2)}) copy-start(f32[128]{0:T(128)} %param.21) | copy-start | bytes 1540
  7.2 44.9 %copy-start.43 = (f32[8]{0:T(128)S(1)}, f32[8]{0:T(128)}, u32[]{:S(2)}) copy-start(f32[8]{0:T(128)} %param.25) | copy-start | bytes 100
  7.2 75.2 %copy-start.26 = (s32[12288]{0:T(1024)S(1)}, s32[12288]{0:T(1024)}, u32[]{:S(2)}) copy-start(s32[12288]{0:T(1024)} %param.19) | copy-start | bytes 147460
  7.2 81.6 %all-gather.17.cloned.1.call-start = ((), (), s32[]{:S(2)}) async-start(), calls=%async_computation.6 | async-start | bytes 1114112 | tf_op jit(solution)/shard_map/all_gather | solution.py:95
  9.0 110.5 %all-gather.15.cloned.1.call-start = ((), (), s32[]{:S(2)}) async-start(), calls=%async_computation.5 | async-start | bytes 1114112 | tf_op jit(solution)/shard_map/all_gather | solution.py:93
  10.6 149.0 %all-gather.19.cloned.1.call-start = ((), (), s32[]{:S(2)}) async-start(), calls=%async_computation.7 | async-start | bytes 1114112 | tf_op jit(solution)/shard_map/all_gather | solution.py:97
  12.2 638.3 %all-gather.25.cloned.1.call-start = ((), (), s32[]{:S(2)}) async-start(), calls=%async_computation.14 | async-start | bytes 56623104 | tf_op jit(solution)/shard_map/all_gather | solution.py:147
  14.7 70.7 %copy-start.22 = (f32[768]{0:T(1024)}, f32[768]{0:T(1024)S(1)}, u32[]{:S(2)}) copy-start(f32[768]{0:T(1024)S(1)} %broadcast_multiply_fusion.1) | copy-start | bytes 9220
  15.7 77.1 %copy-start.24 = (f32[768]{0:T(1024)}, f32[768]{0:T(1024)S(1)}, u32[]{:S(2)}) copy-start(f32[768]{0:T(1024)S(1)} %fusion.37) | copy-start | bytes 9220
  35.9 56.8 %copy-start.20 = (f32[16,1,128]{2,1,0:T(1,128)}, f32[16,1,128]{2,1,0:T(1,128)S(1)}, u32[]{:S(2)}) copy-start(f32[16,1,128]{2,1,0:T(1,128)S(1)} %convert_element_type.334) | copy-start | bytes 24580
  88.9 8.0 copy-start.40
  92.8 31.9 %collective-permute-start = (bf16[768,256]{1,0:T(8,128)(2,1)}, bf16[768,256]{1,0:T(8,128)(2,1)}, u32[]{:S(2)}, u32[]{:S(2)}) collective-permute-start(bf16[768,256]{1,0:T(8,128)(2,1)} %fusion.27), channel_id=1, source_target_pairs={{0,16},{8,24},{16,32},{24,40},{32,48},{40,56},{48,64},{56,72},{64,... | collective-permute-start | bytes 1179656 | tf_op jit(solution)/shard_map/ppermute | solution.py:16
  94.8 29.8 %collective-permute-start.1 = (bf16[768,256]{1,0:T(8,128)(2,1)}, bf16[768,256]{1,0:T(8,128)(2,1)}, u32[]{:S(2)}, u32[]{:S(2)}) collective-permute-start(bf16[768,256]{1,0:T(8,128)(2,1)} %fusion.27), channel_id=1, source_target_pairs={{0,8},{8,16},{16,24},{24,32},{32,40},{40,48},{48,56},{56,64},{64,7... | collective-permute-start | bytes 1179656 | tf_op jit(solution)/shard_map/ppermute | solution.py:16
  124.6 11.2 copy-start.13
  126.1 9.7 copy-start.10
  164.7 19.9 %copy-start.45 = (f32[128]{0:T(128)S(1)}, f32[128]{0:T(128)}, u32[]{:S(2)}) copy-start(f32[128]{0:T(128)} %param.28) | copy-start | bytes 1540
  164.7 37.5 %copy-start.46 = (f32[128]{0:T(128)S(1)}, f32[128]{0:T(128)}, u32[]{:S(2)}) copy-start(f32[128]{0:T(128)} %param.29) | copy-start | bytes 1540
  164.7 53.7 %copy-start.33 = (f32[8,8]{1,0:T(8,128)S(1)}, f32[8,8]{1,0:T(8,128)}, u32[]{:S(2)}) copy-start(f32[8,8]{1,0:T(8,128)} %param.31) | copy-start | bytes 772
  164.7 522.4 %all-gather.21.cloned.1.call-start = ((), (), s32[]{:S(2)}) async-start(), calls=%async_computation.8 | async-start | bytes 4456448 | tf_op jit(solution)/shard_map/all_gather | solution.py:101
  166.6 567.7 %all-gather.23.cloned.1.call-start = ((), (), s32[]{:S(2)}) async-start(), calls=%async_computation.9 | async-start | bytes 4456448 | tf_op jit(solution)/shard_map/all_gather | solution.py:103
  168.4 729.9 %all-reduce.17.cloned.1.call-start = ((), (), s32[]{:S(2)}) async-start(), calls=%async_computation.10 | async-start | bytes 12582912 | tf_op jit(solution)/shard_map/psum | solution.py:163
  237.1 514.5 %copy-start.34 = (f32[1024]{0:T(1024)}, f32[1024]{0:T(1024)S(1)}, u32[]{:S(2)}) copy-start(f32[1024]{0:T(1024)S(1)} %bitcast_convert_fusion) | copy-start | bytes 12292
  734.3 11.7 copy-start.39
  751.4 255.7 %reduce-scatter.20.cloned.1.call-start = ((), (), s32[]{:S(2)}) async-start(), calls=%async_computation.16 | async-start | bytes 4456448
  766.9 265.8 %reduce-scatter.16.cloned.1.call-start = ((), (), s32[]{:S(2)}) async-start(), calls=%async_computation.13 | async-start | bytes 4456448 | tf_op jit(solution)/shard_map/reduce_scatter | solution.py:233
  776.0 321.3 %reduce-scatter.18.cloned.1.call-start = ((), (), s32[]{:S(2)}) async-start(), calls=%async_computation.15 | async-start | bytes 1114112
  898.4 6.5 copy-start.3
  931.7 228.0 %reduce-scatter.12.cloned.1.call-start = ((), (), s32[]{:S(2)}) async-start(), calls=%async_computation.11 | async-start | bytes 1114112 | tf_op jit(solution)/shard_map/reduce_scatter | solution.py:209
  932.0 10.6 copy-start.11
  951.6 5.3 copy-start.14
  962.3 353.3 %all-reduce.19.cloned.1.call-start = ((), (), s32[]{:S(2)}) async-start(), calls=%async_computation.17 | async-start | bytes 13369344 | tf_op jit(solution)/shard_map/psum | solution.py:154
  964.3 13.0 collective-permute-start.2
  965.8 8.9 copy-start.17
  965.8 8.9 copy-start.19
  965.8 19.5 %collective-permute-start.3 = (bf16[768,256]{0,1:T(8,128)(2,1)S(1)}, bf16[768,256]{0,1:T(8,128)(2,1)S(1)}, u32[]{:S(2)}, u32[]{:S(2)}) collective-permute-start(bf16[768,256]{0,1:T(8,128)(2,1)S(1)} %get-tuple-element.45), channel_id=1, source_target_pairs={{16,0},{24,8},{32,16},{40,24},{48,32},{56,40},{64,48},{72,56},{80,... | collective-permute-start | bytes 1179656 | tf_op jit(solution)/shard_map/ppermute | solution.py:16
  974.7 10.7 copy-start.6
  974.7 10.7 copy-start.9
  986.3 20.7 %copy-start.16 = (bf16[1536,128]{1,0:T(8,128)(2,1)S(1)}, bf16[1536,128]{1,0:T(8,128)(2,1)}, u32[]{:S(2)}) copy-start(bf16[1536,128]{1,0:T(8,128)(2,1)} %fusion.24) | copy-start | bytes 1179652
  986.3 455.8 %reduce-scatter.14.cloned.1.call-start = ((), (), s32[]{:S(2)}) async-start(), calls=%async_computation.12 | async-start | bytes 1114112 | tf_op jit(solution)/shard_map/reduce_scatter | solution.py:215
  1009.1 311.6 %copy-start.21 = (f32[16,1,128]{2,1,0:T(1,128)S(1)}, f32[16,1,128]{2,1,0:T(1,128)}, u32[]{:S(2)}) copy-start(f32[16,1,128]{2,1,0:T(1,128)} %copy-done.20) | copy-start | bytes 24580
  1009.1 311.6 %copy-start.23 = (f32[768]{0:T(1024)S(1)}, f32[768]{0:T(1024)}, u32[]{:S(2)}) copy-start(f32[768]{0:T(1024)} %copy-done.22) | copy-start | bytes 9220
  1325.5 61.6 %copy-start.29 = (f32[16,1,128]{2,1,0:T(1,128)S(1)}, f32[16,1,128]{2,1,0:T(1,128)}, u32[]{:S(2)}) copy-start(f32[16,1,128]{2,1,0:T(1,128)} %convert_element_type.339) | copy-start | bytes 24580
  1387.0 6.9 slice-start
  1387.0 6.9 slice-start.1
  1387.1 8.6 copy-start.5
  (20 other events, 63.5 us)
Sparse Core Ops, SparseCore 0:
  10.4 34.8 all-gather.16
  47.5 32.5 all-gather.14
  82.3 40.2 all-gather.18
  164.9 485.6 all-gather.24
  652.1 35.0 all-gather.20
  689.2 44.9 all-gather.22
  751.5 146.8 all-reduce.16
  900.8 64.0 reduce-scatter.19
  967.3 65.4 reduce-scatter.15
  1035.0 62.2 reduce-scatter.17
  1099.8 59.9 reduce-scatter.11
  1162.3 153.2 all-reduce.18
  1385.4 56.6 reduce-scatter.13
